TPU v7x, 512 devices: a whole 4x8x8 slice. The times are simulated.
512 devices in a mesh: phi: 8 (over z), theta: 16 (over y, core), row: 4 (over x).
Axes of the slice: x: 4, y: 8, z: 8, core: 2. Of those that a mesh axis runs over, the one named last changes fastest.
Arguments:
- fields: float32 [8, 12, 1536, 2048], P(None, 'row', 'phi', 'theta'), may hold values from -6 to 6
- kept_counts: int32 [512], replicated, may hold values from 1 to 384, as said below
Outputs:
- filtered: float32 [8, 12, 1536, 2048], P(None, 'row', 'phi', 'theta')
Inputs may be any that keep to these rules, and one draw needn't show every extreme that they name: `kept_counts`: modes 0 to count - 1 of a cap row are kept; some row reaches 384 in every draw.
All inputs are finite; a program needn't handle non-finite values.
Results may differ from a plain program's by a relative error of at most 0.00007.
Values sent between devices are 32-bit elements; how exact they have to be, the bound alone decides.
No kernel may reach another device: no remote copies, remote signals or barrier semaphores. Data moves between devices by JAX's collectives and lax.ppermute only.
A program may use at most 64 MiB of HBM per device.

v0:
```python
import math
import jax
import jax.numpy as jnp
from jax import lax
from jax.sharding import PartitionSpec as P

KMAX = 384


def tables(offset, span_rows, points, mode_count):
    azimuth = offset + jnp.arange(span_rows, dtype=jnp.int32)
    wavenumber = jnp.arange(mode_count, dtype=jnp.int32)
    phase_turns = azimuth[:, None] * wavenumber[None, :] % points
    angles = phase_turns.astype(jnp.float32) * (2.0 * math.pi / points)
    forward = jnp.concatenate([jnp.cos(angles), jnp.sin(angles)], axis=1)
    weight = jnp.where(wavenumber == 0, 1.0, 2.0).astype(jnp.float32) / points
    weight = jnp.concatenate([weight, weight])
    backward = (forward * weight[None, :]).T
    return (forward, backward)


def spectral(lines, row_counts):
    nfields, shells, local_points, rows_here = lines.shape
    n_phi = lax.axis_size("phi")
    points = local_points * n_phi
    highest = lax.Precision.HIGHEST
    groups = nfields * shells
    grouped = lines.reshape(groups, local_points, rows_here)
    line_counts = jnp.broadcast_to(row_counts[None, :], (groups, rows_here)).reshape(-1)
    phi_index = lax.axis_index("phi")
    forward, backward = tables(phi_index * local_points, local_points, points, KMAX)
    share_rows = forward.shape[1] // n_phi
    out = jnp.einsum(
        "pk,gpr->kgr", forward, grouped, precision=highest, preferred_element_type=jnp.float32
    )
    share = lax.psum_scatter(
        out.reshape(share_rows * lax.axis_size("phi"), groups * rows_here),
        "phi",
        scatter_dimension=0,
        tiled=True,
    )
    share_index = phi_index * share_rows + jnp.arange(share_rows, dtype=jnp.int32)
    keep = (share_index % KMAX)[:, None] < line_counts[None, :]
    masked = jnp.where(keep, share, 0.0)
    piece = lax.all_gather(masked, "phi", axis=0, tiled=True)
    stacked = piece.reshape(piece.shape[0], groups, rows_here)
    result = jnp.einsum(
        "kp,kgr->gpr", backward, stacked, precision=highest, preferred_element_type=jnp.float32
    )
    return result.reshape(lines.shape)


def on_device(fields, kept_counts):
    n_theta = lax.axis_size("theta")
    theta_index = lax.axis_index("theta")
    band_rows = fields.shape[3]
    caps = kept_counts.shape[0] // band_rows
    cap_bands = caps // 2
    count_table = kept_counts.reshape(caps, band_rows)
    piece_rows = band_rows // n_theta
    received = lax.all_to_all(fields, "theta", split_axis=3, concat_axis=3, tiled=True)
    north_end = cap_bands * piece_rows
    south_start = (n_theta - cap_bands) * piece_rows
    cap_lines = jnp.concatenate(
        [received[:, :, :, :north_end], received[:, :, :, south_start:]], axis=3
    )
    row_counts = lax.dynamic_slice_in_dim(
        count_table, theta_index * piece_rows, piece_rows, 1
    ).reshape(-1)
    smoothed = spectral(cap_lines, row_counts)
    rebuilt = jnp.concatenate(
        [
            smoothed[:, :, :, :north_end],
            received[:, :, :, north_end:south_start],
            smoothed[:, :, :, north_end:],
        ],
        axis=3,
    )
    return lax.all_to_all(rebuilt, "theta", split_axis=3, concat_axis=3, tiled=True)


def solution(mesh):
    placed = (P(None, "row", "phi", "theta"), P())
    return jax.shard_map(
        on_device,
        mesh=mesh,
        in_specs=placed,
        out_specs=P(None, "row", "phi", "theta"),
        check_vma=False,
    )
```

profile of v0, /device:TPU:1, one launch (start us, length us, event | category | flops | bytes accessed | tf_op | source)
XLA Modules:
  0.0 286.2 jit_solution(12094316669807166460)
XLA Ops:
  6.5 3.6 %copy.26 = f32[8,3,192,128]{2,0,1,3:T(8,128)} copy(f32[8,3,192,128]{3,2,1,0:T(8,128)} %param.2) | data formatting | bytes 4718592 | tf_op args[0]
  10.1 10.4 %all-to-all-start = ((f32[8,3,192,128]{2,0,1,3:T(8,128)}), f32[8,3,192,128]{2,0,1,3:T(8,128)S(1)}, u32[]{:S(2)}, u32[]{:S(2)}) async-start(f32[8,3,192,128]{2,0,1,3:T(8,128)} %copy.26), calls=%async_computation | async-start | bytes 6291456 | tf_op jit(solution)/shard_map/all_to_all | solution.py:61
  20.5 2.1 fusion.10
  22.6 68.9 %all-to-all-done = f32[8,3,192,128]{2,0,1,3:T(8,128)S(1)} async-done(((f32[8,3,192,128]{2,0,1,3:T(8,128)}), f32[8,3,192,128]{2,0,1,3:T(8,128)S(1)}, u32[]{:S(2)}, u32[]{:S(2)}) %all-to-all-start) | async-done | bytes 2359328 | tf_op jit(solution)/shard_map/all_to_all | solution.py:61
  91.5 0.1 copy.27
  91.7 0.1 copy.28
  91.8 0.1 pad_maximum_fusion.1
  91.9 0.7 copy-done.2
  92.6 5.4 %fusion.3 = f32[768,768]{1,0:T(8,128)} fusion(f32[768,192]{1,0:T(8,128)S(1)} %bitcast.17, f32[192,384]{1,0:T(8,128)S(1)} %copy-done.2, f32[192,384]{1,0:T(8,128)S(1)} %get-tuple-element.9), kind=kOutput, calls=%fused_computation.6 | convolution fusion | flops 1359101952 | bytes 3538944 | tf_op jit(solution)/shard_map/pk,gpr->kgr/dot_general | solution.py:33
  98.1 0.1 constant_dynamic-slice_fusion
  98.1 0.1 broadcast_in_dim.23
  98.2 0.1 lt.33
  98.3 42.2 %reduce-scatter.2.cloned.1.call-done = f32[96,768]{1,0:T(8,128)} async-done(((f32[768,768]{1,0:T(8,128)}), f32[96,768]{1,0:T(8,128)}) %reduce-scatter.2.cloned.1.call-update) | async-done | bytes 294928 | tf_op jit(solution)/shard_map/reduce_scatter | solution.py:36
  140.5 1.8 compare_select_fusion
  142.3 44.4 %all-gather.2.cloned.1.call-done = f32[768,768]{1,0:T(8,128)} async-done(((f32[96,768]{1,0:T(8,128)}), f32[768,768]{1,0:T(8,128)}) %all-gather.2.cloned.1.call-update) | async-done | bytes 2359312 | tf_op jit(solution)/shard_map/all_gather | solution.py:45
  186.7 2.0 copy.29
  188.8 2.0 fusion
  190.8 0.1 fusion.15
  190.9 0.2 copy.33
  191.1 0.2 copy.34
  191.4 1.1 slice-done
  192.5 0.2 pad_maximum_fusion
  192.7 84.5 %all_to_all.10 = f32[8,3,192,128]{2,0,1,3:T(8,128)S(1)} all-to-all(f32[8,3,192,128]{2,0,1,3:T(8,128)S(1)} %pad_maximum_fusion), channel_id=1, replica_groups=mesh['phi'=8,'theta'=16,'row'=4] {'theta'}, dimensions={3} | all-to-all | bytes 4718592 | tf_op jit(solution)/shard_map/all_to_all | solution.py:79
  277.2 2.1 copy.32
  (18 shorter events, 0.2 us)
Async XLA Ops:
  6.5 91.5 %copy-start = (s32[512]{0:T(512)S(1)}, s32[512]{0:T(512)}, u32[]{:S(2)}) copy-start(s32[512]{0:T(512)} %param.3) | copy-start | bytes 6148
  10.1 81.4 %all-to-all-start = ((f32[8,3,192,128]{2,0,1,3:T(8,128)}), f32[8,3,192,128]{2,0,1,3:T(8,128)S(1)}, u32[]{:S(2)}, u32[]{:S(2)}) async-start(f32[8,3,192,128]{2,0,1,3:T(8,128)} %copy.26), calls=%async_computation | async-start | bytes 6291456 | tf_op jit(solution)/shard_map/all_to_all | solution.py:61
  20.5 120.0 %reduce-scatter.2.cloned.1.call-start = ((), (), s32[]{:S(2)}) async-start(), calls=%async_computation.3 | async-start | bytes 2654208 | tf_op jit(solution)/shard_map/reduce_scatter | solution.py:36
  91.5 50.8 %copy-start.1 = (f32[8,3,192,128]{2,0,1,3:T(8,128)}, f32[8,3,192,128]{2,0,1,3:T(8,128)S(1)}, u32[]{:S(2)}) copy-start(f32[8,3,192,128]{2,0,1,3:T(8,128)S(1)} %all-to-all-done) | copy-start | bytes 7077892
  91.5 1.2 copy-start.2
  98.0 88.7 %all-gather.2.cloned.1.call-start = ((), (), s32[]{:S(2)}) async-start(), calls=%async_computation.4 | async-start | bytes 2654208 | tf_op jit(solution)/shard_map/all_gather | solution.py:45
  142.3 46.5 %copy-start.3 = (f32[192,384]{1,0:T(8,128)S(1)}, f32[192,384]{1,0:T(8,128)}, u32[]{:S(2)}) copy-start(f32[192,384]{1,0:T(8,128)} %get-tuple-element.10) | copy-start | bytes 884740
  190.8 1.7 slice-start
Sparse Core Ops, SparseCore 0:
  98.1 42.3 reduce-scatter.1
  142.6 44.1 all-gather.1
where the time goes:
time: 286 us
  waiting for transfers between devices  155 us (54%)
  blocking collectives  84.5 us (30%)
  between operations  13.6 us (5%)
  local copies, waits for them, and re-layouts  10.6 us (4%)
  starting transfers between devices  10.4 us (4%)
  matrix products  7.4 us (3%)
  other arithmetic  4.12 us (1%)
    all_to_all x1, blocking collectives, on_device(): lax.all_to_all(rebuilt, 'theta', split_axis=3, concat_axis=3, tiled=True)  84.5 us
    all_to_all x1, waiting for transfers between devices, on_device(): lax.all_to_all(fields, 'theta', split_axis=3, concat_axis=3, tiled=True)  68.9 us
    all_gather x1, waiting for transfers between devices, spectral(): piece = lax.all_gather(masked, 'phi', axis=0, tiled=True)  44.4 us
    reduce_scatter x1, waiting for transfers between devices, spectral(): lax.psum_scatter(out.reshape(share_rows * lax.axis_size('phi'), groups *...  42.2 us
    all_to_all x1, starting transfers between devices, on_device(): lax.all_to_all(fields, 'theta', split_axis=3, concat_axis=3, tiled=True)  10.4 us
  transfers between devices with their start and end apart: 3, of which 3 were waited for; matrix products, arithmetic and copies ran while one was open for 1% of the time, Pallas kernels for 0%

commit v1 on v0

--- a/solution.py
+++ b/solution.py
@@ -42,7 +42,9 @@
     share_index = phi_index * share_rows + jnp.arange(share_rows, dtype=jnp.int32)
     keep = (share_index % KMAX)[:, None] < line_counts[None, :]
     masked = jnp.where(keep, share, 0.0)
-    piece = lax.all_gather(masked, "phi", axis=0, tiled=True)
+    piece = jnp.concatenate(
+        lax.all_to_all(jnp.stack([masked] * lax.axis_size("phi")), "phi", 0, 0), axis=0
+    )
     stacked = piece.reshape(piece.shape[0], groups, rows_here)
     result = jnp.einsum(
         "kp,kgr->gpr", backward, stacked, precision=highest, preferred_element_type=jnp.float32

time: 286 us -> 306 us (1.070)
  waiting for transfers between devices: 155 us -> 164 us
  starting transfers between devices: 10.4 us -> 15.7 us
  local copies, waits for them, and re-layouts: 10.6 us -> 14.7 us
    all_to_all x0 -> x1, waiting for transfers between devices: none -> 52.9 us  [spectral(): lax.all_to_all(jnp.stack([masked] * lax.axis_size('phi')), 'phi', 0, 0)]
    all_gather x1 -> x0, waiting for transfers between devices: 44.4 us -> none  [spectral(): piece = lax.all_gather(masked, 'phi', axis=0, tiled=True)]
    all_to_all x0 -> x1, starting transfers between devices: none -> 5.34 us  [spectral(): lax.all_to_all(jnp.stack([masked] * lax.axis_size('phi')), 'phi', 0, 0)]
    another operation x0 -> x2, local copies, waits for them, and re-layouts: none -> 3.64 us  [the longest x1 2.04 us: spectral(): stacked = piece.reshape(piece.shape[0], groups, rows_here)]
where the time goes in v1:
time: 306 us; the launch traced here: 305 us
  waiting for transfers between devices  164 us (54%)
  blocking collectives  85 us (28%)
  starting transfers between devices  15.7 us (5%)
  local copies, waits for them, and re-layouts  14.7 us (5%)
  between operations  13.5 us (4%)
  matrix products  9.06 us (3%)
  other arithmetic  3.41 us (1%)
    all_to_all x1, blocking collectives, on_device(): lax.all_to_all(rebuilt, 'theta', split_axis=3, concat_axis=3, tiled=True)  85 us
    all_to_all x1, waiting for transfers between devices, on_device(): lax.all_to_all(fields, 'theta', split_axis=3, concat_axis=3, tiled=True)  68.9 us
    all_to_all x1, waiting for transfers between devices, spectral(): lax.all_to_all(jnp.stack([masked] * lax.axis_size('phi')), 'phi', 0, 0)  52.9 us
    reduce_scatter x1, waiting for transfers between devices, spectral(): lax.psum_scatter(out.reshape(share_rows * lax.axis_size('phi'), groups *...  42 us
    all_to_all x1, starting transfers between devices, on_device(): lax.all_to_all(fields, 'theta', split_axis=3, concat_axis=3, tiled=True)  10.4 us
  transfers between devices with their start and end apart: 3, of which 3 were waited for; matrix products, arithmetic and copies ran while one was open for 1% of the time, Pallas kernels for 0%

profile of v1, /device:TPU:1, one launch (start us, length us, event | category | flops | bytes accessed | tf_op | source)
XLA Modules:
  0.0 305.2 jit_solution(6784652926554864327)
XLA Ops:
  6.5 3.6 %copy.26 = f32[8,3,192,128]{2,0,1,3:T(8,128)} copy(f32[8,3,192,128]{3,2,1,0:T(8,128)} %param.2) | data formatting | bytes 4718592 | tf_op args[0]
  10.1 10.4 %all-to-all-start = ((f32[8,3,192,128]{2,0,1,3:T(8,128)}), f32[8,3,192,128]{2,0,1,3:T(8,128)S(1)}, u32[]{:S(2)}, u32[]{:S(2)}) async-start(f32[8,3,192,128]{2,0,1,3:T(8,128)} %copy.26), calls=%async_computation | async-start | bytes 6291456 | tf_op jit(solution)/shard_map/all_to_all | solution.py:63
  20.5 2.1 fusion.10
  22.6 68.9 %all-to-all-done = f32[8,3,192,128]{2,0,1,3:T(8,128)S(1)} async-done(((f32[8,3,192,128]{2,0,1,3:T(8,128)}), f32[8,3,192,128]{2,0,1,3:T(8,128)S(1)}, u32[]{:S(2)}, u32[]{:S(2)}) %all-to-all-start) | async-done | bytes 2359328 | tf_op jit(solution)/shard_map/all_to_all | solution.py:63
  91.5 0.1 copy.27
  91.7 0.1 copy.28
  91.9 0.7 copy-done.2
  92.6 5.4 %fusion.3 = f32[768,768]{1,0:T(8,128)} fusion(f32[768,192]{1,0:T(8,128)S(1)} %bitcast.17, f32[192,384]{1,0:T(8,128)S(1)} %copy-done.2, f32[192,384]{1,0:T(8,128)S(1)} %get-tuple-element.9), kind=kOutput, calls=%fused_computation.6 | convolution fusion | flops 1359101952 | bytes 3538944 | tf_op jit(solution)/shard_map/pk,gpr->kgr/dot_general | solution.py:33
  98.0 0.1 constant_dynamic-slice_fusion
  98.1 0.1 broadcast_in_dim.23
  98.3 42.0 %reduce-scatter.2.cloned.1.call-done = f32[96,768]{1,0:T(8,128)} async-done(((f32[768,768]{1,0:T(8,128)}), f32[96,768]{1,0:T(8,128)}) %reduce-scatter.2.cloned.1.call-update) | async-done | bytes 294928 | tf_op jit(solution)/shard_map/reduce_scatter | solution.py:36
  140.3 1.0 compare_select_fusion
  141.3 1.6 stack.2
  142.9 5.3 %all-to-all-start.1 = ((f32[8,96,768]{2,1,0:T(8,128)}), f32[8,96,768]{2,1,0:T(8,128)}, u32[]{:S(2)}, u32[]{:S(2)}) async-start(f32[8,96,768]{2,1,0:T(8,128)} %stack.2), calls=%async_computation.2 | async-start | bytes 4718592 | tf_op jit(solution)/shard_map/all_to_all | solution.py:46
  148.3 52.9 %all-to-all-done.1 = f32[8,96,768]{2,1,0:T(8,128)} async-done(((f32[8,96,768]{2,1,0:T(8,128)}), f32[8,96,768]{2,1,0:T(8,128)}, u32[]{:S(2)}, u32[]{:S(2)}) %all-to-all-start.1) | async-done | bytes 2359328 | tf_op jit(solution)/shard_map/all_to_all | solution.py:46
  201.2 2.5 copy.29
  203.7 2.0 reshape_reshape.3
  205.7 3.7 %fusion = f32[24,32,192]{2,1,0:T(8,128)S(1)} fusion(f32[768,24,32]{0,2,1:T(8,128)} %reshape_reshape.3, f32[192,384]{1,0:T(8,128)} %get-tuple-element.10, f32[192,384]{1,0:T(8,128)S(1)} %get-tuple-element.9, f32[768]{0:T(1024)S(1)} %pad_maximum_fusion.5), kind=kOutput, calls=%fused_computation.3 | convolution fusion | flops 1359249408 | bytes 3542016 | tf_op jit(solution)/shard_map/kp,kgr->gpr/dot_general | solution.py:49
  209.5 0.2 copy.33
  209.7 0.2 copy.34
  210.0 1.1 slice-done
  211.1 0.2 pad_maximum_fusion
  211.3 85.0 %all_to_all.15 = f32[8,3,192,128]{2,0,1,3:T(8,128)S(1)} all-to-all(f32[8,3,192,128]{2,0,1,3:T(8,128)S(1)} %pad_maximum_fusion), channel_id=1, replica_groups=mesh['phi'=8,'theta'=16,'row'=4] {'theta'}, dimensions={3} | all-to-all | bytes 4718592 | tf_op jit(solution)/shard_map/all_to_all | solution.py:81
  296.2 2.1 copy.32
  (17 shorter events, 0.3 us)
Async XLA Ops:
  6.5 91.5 %copy-start = (s32[512]{0:T(512)S(1)}, s32[512]{0:T(512)}, u32[]{:S(2)}) copy-start(s32[512]{0:T(512)} %param.3) | copy-start | bytes 6148
  10.1 81.4 %all-to-all-start = ((f32[8,3,192,128]{2,0,1,3:T(8,128)}), f32[8,3,192,128]{2,0,1,3:T(8,128)S(1)}, u32[]{:S(2)}, u32[]{:S(2)}) async-start(f32[8,3,192,128]{2,0,1,3:T(8,128)} %copy.26), calls=%async_computation | async-start | bytes 6291456 | tf_op jit(solution)/shard_map/all_to_all | solution.py:63
  20.5 119.8 %reduce-scatter.2.cloned.1.call-start = ((), (), s32[]{:S(2)}) async-start(), calls=%async_computation.4 | async-start | bytes 2654208 | tf_op jit(solution)/shard_map/reduce_scatter | solution.py:36
  91.5 56.9 %copy-start.1 = (f32[8,3,192,128]{2,0,1,3:T(8,128)}, f32[8,3,192,128]{2,0,1,3:T(8,128)S(1)}, u32[]{:S(2)}) copy-start(f32[8,3,192,128]{2,0,1,3:T(8,128)S(1)} %all-to-all-done) | copy-start | bytes 7077892
  91.5 1.2 copy-start.2
  142.9 58.2 %all-to-all-start.1 = ((f32[8,96,768]{2,1,0:T(8,128)}), f32[8,96,768]{2,1,0:T(8,128)}, u32[]{:S(2)}, u32[]{:S(2)}) async-start(f32[8,96,768]{2,1,0:T(8,128)} %stack.2), calls=%async_computation.2 | async-start | bytes 4718592 | tf_op jit(solution)/shard_map/all_to_all | solution.py:46
  209.4 1.7 slice-start
Sparse Core Ops, SparseCore 0:
  98.1 42.1 reduce-scatter.1
